TPU v7x, 256 devices: a whole 4x4x8 slice. The times are simulated.
256 devices in a mesh: section: 2 (over y_hi), segment: 8 (over x, core), fsdp: 16 (over z, y_lo).
Axes of the slice: x: 4, y: 4 (y_hi: 2, y_lo: 2; y = y_hi * 2 + y_lo), z: 8, core: 2. Of those that a mesh axis runs over, the one named last changes fastest.
Arguments:
- out_grad: bfloat16 [2, 16, 256, 6144], P(None, 'fsdp'), may hold values from -48 to 48
- queries: bfloat16 [2, 16, 256, 6144], P(None, 'fsdp', None, 'segment'), may hold values from -40 to 40
- enc_keys: bfloat16 [2, 16, 256, 6144], P(None, 'fsdp', None, 'segment'), may hold values from -4 to 4
- enc_values: bfloat16 [2, 16, 256, 6144], P(None, 'fsdp', None, 'segment'), may hold values from -6 to 6
- key_mask: int32 [2, 16, 256], P(None, 'fsdp'), may hold values from 0 to 1, as said below
- weights: bfloat16 [2, 2, 6144, 6144], P('section', None, 'fsdp', 'segment'), may hold values from -0.078125 to 0.078125
Outputs:
- grads: bfloat16 [2, 2, 16, 256, 6144], P('section', None, 'fsdp', None, 'segment')
Inputs may be any that keep to these rules, and one draw needn't show every extreme that they name: `key_mask`: each row is 1 on a prefix of 128 or more positions and 0 after it; the first reaction of every microbatch has no padding.
All inputs are finite; a program needn't handle non-finite values.
Results may differ from a plain program's by a relative error of at most 0.014.
Values may be sent and summed in bfloat16 or wider, within the bound.
No kernel may reach another device: no remote copies, remote signals or barrier semaphores. Data moves between devices by JAX's collectives and lax.ppermute only.
A program may use at most 128 MiB of HBM per device.

v0:
```python
import jax
import jax.numpy as jnp
from jax import lax
from jax.sharding import PartitionSpec as P

HDIM = 128


def passed_along(value, axis, by):
    peers = lax.axis_size(axis)
    pairs = [(i, i + by) for i in range(peers) if 0 <= i + by < peers]
    return lax.ppermute(value, axis, pairs)


def attend(grad_rows, first_weight, queries, enc_keys, enc_values, key_mask):
    reaction_count, seq_length, local_width = queries.shape
    head_count = local_width // HDIM
    score_scale = HDIM ** (-0.5)
    ctx_grad = jnp.dot(grad_rows, first_weight, preferred_element_type=jnp.float32).astype(
        jnp.bfloat16
    )
    shaped = (reaction_count, seq_length, head_count, HDIM)
    grad_heads = ctx_grad.reshape(shaped)
    query_heads = queries.reshape(shaped)
    key_heads = enc_keys.reshape(shaped)
    value_heads = enc_values.reshape(shaped)
    scores = (
        jnp.einsum("bihc,bjhc->bhij", query_heads, key_heads, preferred_element_type=jnp.float32)
        * score_scale
    )
    scores = jnp.where(key_mask[:, None, None, :] > 0, scores, -jnp.inf)
    row_top = jnp.max(scores, axis=-1, keepdims=True)
    exp_scores = jnp.exp(scores - row_top)
    probabilities = exp_scores / jnp.sum(exp_scores, axis=-1, keepdims=True)
    probs_half = probabilities.astype(jnp.bfloat16)
    prob_grad = jnp.einsum(
        "bihc,bjhc->bhij", grad_heads, value_heads, preferred_element_type=jnp.float32
    )
    center = jnp.sum(probabilities * prob_grad, axis=-1, keepdims=True)
    score_grad = (probabilities * (prob_grad - center)).astype(jnp.bfloat16)
    query_grad = (
        jnp.einsum("bhij,bjhc->bihc", score_grad, key_heads, preferred_element_type=jnp.float32)
        * score_scale
    ).astype(jnp.bfloat16)
    key_grad = (
        jnp.einsum("bhij,bihc->bjhc", score_grad, query_heads, preferred_element_type=jnp.float32)
        * score_scale
    ).astype(jnp.bfloat16)
    value_grad = jnp.einsum(
        "bhij,bihc->bjhc", probs_half, grad_heads, preferred_element_type=jnp.float32
    ).astype(jnp.bfloat16)
    flat = (reaction_count * seq_length, local_width)
    return (query_grad.reshape(flat), key_grad.reshape(flat), value_grad.reshape(flat))


def project(grad_rows, weight_cols):
    return lax.dot_general(
        grad_rows, weight_cols, (((1,), (1,)), ((), ())), preferred_element_type=jnp.float32
    )


def per_device(out_grad, queries, enc_keys, enc_values, key_mask, weights):
    decoder = lax.axis_index("section") == 1
    gathered = lax.all_gather(weights, "fsdp", axis=2, tiled=True)
    first_weight = gathered[0, 0]
    second_weight = gathered[0, 1]
    micro_count, reaction_count, seq_length, feature_width = out_grad.shape
    local_width = queries.shape[3]
    row_count = micro_count * reaction_count * seq_length
    flat = (micro_count * reaction_count, seq_length, local_width)

    def decoder_work():
        return attend(
            out_grad.reshape(row_count, feature_width),
            first_weight,
            queries.reshape(flat),
            enc_keys.reshape(flat),
            enc_values.reshape(flat),
            key_mask.reshape(micro_count * reaction_count, seq_length),
        )

    def encoder_work():
        blank_grads = jnp.zeros((row_count, local_width), jnp.bfloat16)
        return (blank_grads, blank_grads, blank_grads)

    query_grad, key_grad, value_grad = lax.cond(decoder, decoder_work, encoder_work)
    got_keys, got_values = passed_along((key_grad, value_grad), "section", -1)
    partial_sum = lax.cond(
        decoder,
        lambda: project(query_grad, second_weight),
        lambda: project(got_keys, first_weight) + project(got_values, second_weight),
    )
    summed = lax.psum_scatter(
        partial_sum.astype(jnp.bfloat16), "segment", scatter_dimension=1, tiled=True
    ).astype(jnp.float32)
    result = summed.astype(jnp.bfloat16).reshape(
        1, micro_count, reaction_count, seq_length, summed.shape[1]
    )
    return result


def solution(mesh):
    return jax.shard_map(
        per_device,
        mesh=mesh,
        in_specs=(
            P(None, "fsdp", None, None),
            P(None, "fsdp", None, "segment"),
            P(None, "fsdp", None, "segment"),
            P(None, "fsdp", None, "segment"),
            P(None, "fsdp", None),
            P("section", None, "fsdp", "segment"),
        ),
        out_specs=P("section", None, "fsdp", None, "segment"),
        check_vma=False,
    )
```

profile of v0, /device:TPU:1, one launch (start us, length us, event | category | flops | bytes accessed | tf_op | source)
XLA Modules:
  0.0 565.3 jit_solution(8359995170980936187)
XLA Ops:
  6.5 0.0 all-gather.2.cloned.1.call-start
  6.5 0.7 all-gather.2.cloned.1.call-update
  7.3 0.0 reduce-scatter.2.cloned.1.call-start
  7.3 0.0 copy-start.3
  7.3 0.0 copy-start.5
  7.3 398.5 %all-gather.2.cloned.1.call-done = bf16[1,2,6144,768]{3,2,1,0:T(8,128)(2,1)} async-done(((bf16[1,2,384,768]{3,2,1,0:T(8,128)(2,1)}), bf16[1,2,6144,768]{3,2,1,0:T(8,128)(2,1)}) %all-gather.2.cloned.1.call-update) | async-done | bytes 18874384 | tf_op jit(solution)/shard_map/all_gather | solution.py:64
  405.9 14.6 %slice_bitcast_fusion = (bf16[6144,768]{1,0:T(8,128)(2,1)}, bf16[6144,768]{1,0:T(8,128)(2,1)}) fusion(bf16[1,2,6144,768]{3,2,1,0:T(8,128)(2,1)} %all-gather.2.cloned.1.call-done), kind=kLoop, calls=%fused_computation.24 | loop fusion | bytes 37748736 | tf_op jit(solution)/shard_map/squeeze | solution.py:66
  420.5 0.0 copy-done.3
  420.5 0.0 copy-done.5
  420.5 1.1 conditional.2
  420.5 0.1 broadcast.21.clone.1
  420.5 0.1 broadcast.21.clone
  420.6 0.9 broadcast.21
  421.5 0.3 copy.39
  421.8 0.3 copy.40
  422.1 1.3 collective-permute-start.1
  423.4 1.3 collective-permute-start
  424.7 43.1 %collective-permute-done.1 = bf16[512,768]{1,0:T(8,128)(2,1)S(1)} collective-permute-done((bf16[512,768]{1,0:T(8,128)(2,1)S(1)}, bf16[512,768]{1,0:T(8,128)(2,1)S(1)}, u32[]{:S(2)}, u32[]{:S(2)}) %collective-permute-start.1) | collective-permute-done | bytes 786464 | tf_op jit(solution)/shard_map/ppermute | solution.py:12
  467.8 16.9 %collective-permute-done = bf16[512,768]{1,0:T(8,128)(2,1)S(1)} collective-permute-done((bf16[512,768]{1,0:T(8,128)(2,1)S(1)}, bf16[512,768]{1,0:T(8,128)(2,1)S(1)}, u32[]{:S(2)}, u32[]{:S(2)}) %collective-permute-start) | collective-permute-done | bytes 786464 | tf_op jit(solution)/shard_map/ppermute | solution.py:12
  484.6 24.2 %conditional.3 = (bf16[512,6144]{1,0:T(8,128)(2,1)}) conditional(s32[]{:T(128)} %convert_element_type.36, (bf16[512,768]{1,0:T(8,128)(2,1)S(1)}, bf16[6144,768]{1,0:T(8,128)(2,1)}, bf16[512,768]{1,0:T(8,128)(2,1)S(1)}, bf16[6144,768]{1,0:T(8,128)(2,1)}) %tuple.21, (bf16[512,768]{0,1:T(8,128)(2,1)}, bf16[6144,768]{1,0:T(8,128)(2,1)}) %tuple.22), branch_computations={%region_5.6_spmd, %region_6.7_spmd} | conditional | flops 9669967872 | bytes 51904520 | solution.py:88
  484.6 11.6 %fusion.21 = f32[512,6144]{1,0:T(8,128)} fusion(bf16[512,768]{1,0:T(8,128)(2,1)S(1)} %get-tuple-element.38, bf16[6144,768]{1,0:T(8,128)(2,1)} %get-tuple-element.39), kind=kOutput, calls=%fused_computation.28 | convolution fusion | flops 4831838208 | bytes 22806528 | tf_op jit(solution)/shard_map/cond/branch_0_fun/dot_general | solution.py:57
  496.2 12.6 %convolution_add_fusion = bf16[512,6144]{1,0:T(8,128)(2,1)} fusion(f32[512,6144]{1,0:T(8,128)} %fusion.21, bf16[512,768]{1,0:T(8,128)(2,1)S(1)} %get-tuple-element.40, bf16[6144,768]{1,0:T(8,128)(2,1)} %get-tuple-element.41), kind=kOutput, calls=%fused_computation.23 | convolution fusion | flops 4838129664 | bytes 29097984 | tf_op jit(solution)/shard_map/cond/branch_0_fun/dot_general | solution.py:57
  508.8 0.0 reduce-scatter.2.cloned.1.call-update
  508.9 49.6 %reduce-scatter.2.cloned.1.call-done = bf16[512,768]{1,0:T(8,128)(2,1)} async-done(((bf16[512,6144]{1,0:T(8,128)(2,1)}), bf16[512,768]{1,0:T(8,128)(2,1)}) %reduce-scatter.2.cloned.1.call-update) | async-done | bytes 786448 | tf_op jit(solution)/shard_map/reduce_scatter | solution.py:93
Async XLA Ops:
  6.5 399.3 %all-gather.2.cloned.1.call-start = ((), (), s32[]{:S(2)}) async-start(), calls=%async_computation.1 | async-start | bytes 20054016 | tf_op jit(solution)/shard_map/all_gather | solution.py:64
  7.3 551.2 %reduce-scatter.2.cloned.1.call-start = ((), (), s32[]{:S(2)}) async-start(), calls=%async_computation.2 | async-start | bytes 7077888 | tf_op jit(solution)/shard_map/reduce_scatter | solution.py:93
  7.3 413.2 %copy-start.3 = (bf16[2,1,256,768]{3,2,1,0:T(8,128)(2,1)S(1)}, bf16[2,1,256,768]{3,2,1,0:T(8,128)(2,1)}, u32[]{:S(2)}) copy-start(bf16[2,1,256,768]{3,2,1,0:T(8,128)(2,1)} %param.13) | copy-start | bytes 2359300
  7.3 413.1 %copy-start.5 = (s32[2,1,256]{2,1,0:T(1,128)S(1)}, s32[2,1,256]{2,1,0:T(1,128)}, u32[]{:S(2)}) copy-start(s32[2,1,256]{2,1,0:T(1,128)} %param.14) | copy-start | bytes 6148
  422.1 45.7 %collective-permute-start.1 = (bf16[512,768]{1,0:T(8,128)(2,1)S(1)}, bf16[512,768]{1,0:T(8,128)(2,1)S(1)}, u32[]{:S(2)}, u32[]{:S(2)}) collective-permute-start(bf16[512,768]{1,0:T(8,128)(2,1)S(1)} %copy.40), channel_id=1, source_target_pairs={{128,0},{129,1},{130,2},{131,3},{132,4},{133,5},{134,6},{135,7},{1... | collective-permute-start | bytes 2359304 | tf_op jit(solution)/shard_map/ppermute | solution.py:12
  423.4 61.2 %collective-permute-start = (bf16[512,768]{1,0:T(8,128)(2,1)S(1)}, bf16[512,768]{1,0:T(8,128)(2,1)S(1)}, u32[]{:S(2)}, u32[]{:S(2)}) collective-permute-start(bf16[512,768]{1,0:T(8,128)(2,1)S(1)} %copy.39), channel_id=1, source_target_pairs={{128,0},{129,1},{130,2},{131,3},{132,4},{133,5},{134,6},{135,7},{1... | collective-permute-start | bytes 2359304 | tf_op jit(solution)/shard_map/ppermute | solution.py:12
Sparse Core Ops, SparseCore 0:
  9.1 396.7 all-gather.1
  509.0 49.4 reduce-scatter.1
where the time goes:
time: 565 us
  waiting for transfers between devices  509 us (90%)
  matrix products  24.2 us (4%)
  local copies, waits for them, and re-layouts  16.2 us (3%)
  between operations  13.5 us (2%)
    all_gather x1, waiting for transfers between devices, per_device(): gathered = lax.all_gather(weights, 'fsdp', axis=2, tiled=True)  399 us
    ppermute x2, waiting for transfers between devices, passed_along(): return lax.ppermute(value, axis, pairs)  59.9 us
    reduce_scatter x1, waiting for transfers between devices, per_device(): lax.psum_scatter(partial_sum.astype(jnp.bfloat16), 'segment', scatter_dim...  49.6 us
    dot_general x2, matrix products, project(): lax.dot_general(grad_rows, weight_cols, (((1,), (1,)), ((), ())), preferr...  24.2 us
    squeeze x1, local copies, waits for them, and re-layouts, per_device(): second_weight = gathered[0, 1]  14.6 us
  transfers between devices with their start and end apart: 4, of which 4 were waited for; matrix products, arithmetic and copies ran while one was open for 0% of the time, Pallas kernels for 0%

commit v1 on v0

--- a/solution.py
+++ b/solution.py
@@ -61,7 +61,9 @@
 
 def per_device(out_grad, queries, enc_keys, enc_values, key_mask, weights):
     decoder = lax.axis_index("section") == 1
-    gathered = lax.all_gather(weights, "fsdp", axis=2, tiled=True)
+    gathered = jnp.concatenate(
+        lax.all_to_all(jnp.stack([weights] * lax.axis_size("fsdp")), "fsdp", 0, 0), axis=2
+    )
     first_weight = gathered[0, 0]
     second_weight = gathered[0, 1]
     micro_count, reaction_count, seq_length, feature_width = out_grad.shape

time: 565 us -> 608 us (1.076)
  waiting for transfers between devices: 509 us -> 532 us
  starting transfers between devices: 2.62 us -> 12.8 us
  local copies, waits for them, and re-layouts: 16.2 us -> 25.6 us
    all_to_all x0 -> x1, waiting for transfers between devices: none -> 431 us  [per_device(): lax.all_to_all(jnp.stack([weights] * lax.axis_size('fsdp')), 'fsdp', 0, 0)]
    all_gather x1 -> x0, waiting for transfers between devices: 399 us -> none  [per_device(): gathered = lax.all_gather(weights, 'fsdp', axis=2, tiled=True)]
    all_to_all x0 -> x1, starting transfers between devices: none -> 10.2 us  [per_device(): lax.all_to_all(jnp.stack([weights] * lax.axis_size('fsdp')), 'fsdp', 0, 0)]
    all_to_all x0 -> x1, local copies, waits for them, and re-layouts: none -> 9.76 us  [per_device(): lax.all_to_all(jnp.stack([weights] * lax.axis_size('fsdp')), 'fsdp', 0, 0)]
    squeeze x1, local copies, waits for them, and re-layouts: 14.6 us -> 6.63 us  [per_device(): second_weight = gathered[0, 1]]
    reduce_scatter x1, waiting for transfers between devices: 49.6 us -> 41.7 us  [per_device(): lax.psum_scatter(partial_sum.astype(jnp.bfloat16), 'segment', scatter_dim...]
    another operation x3 -> x4, local copies, waits for them, and re-layouts: 1.04 us -> 8.69 us  [the longest x1 7.65 us: per_device(): jnp.stack([weights] * lax.axis_size('fsdp'))]
where the time goes in v1:
time: 608 us
  waiting for transfers between devices  532 us (88%)
  local copies, waits for them, and re-layouts  25.6 us (4%)
  matrix products  24.2 us (4%)
  between operations  13.5 us (2%)
  starting transfers between devices  12.8 us (2%)
    all_to_all x1, waiting for transfers between devices, per_device(): lax.all_to_all(jnp.stack([weights] * lax.axis_size('fsdp')), 'fsdp', 0, 0)  431 us
    ppermute x2, waiting for transfers between devices, passed_along(): return lax.ppermute(value, axis, pairs)  59.6 us
    reduce_scatter x1, waiting for transfers between devices, per_device(): lax.psum_scatter(partial_sum.astype(jnp.bfloat16), 'segment', scatter_dim...  41.7 us
    dot_general x2, matrix products, project(): lax.dot_general(grad_rows, weight_cols, (((1,), (1,)), ((), ())), preferr...  24.2 us
  transfers between devices with their start and end apart: 4, of which 4 were waited for; matrix products, arithmetic and copies ran while one was open for 0% of the time, Pallas kernels for 0%

profile of v1, /device:TPU:1, one launch (start us, length us, event | category | flops | bytes accessed | tf_op | source)
XLA Modules:
  0.0 608.1 jit_solution(4045729082495823688)
XLA Ops:
  6.5 7.6 %stack.2 = bf16[16,1,2,384,768]{4,3,2,1,0:T(8,128)(2,1)} broadcast(bf16[2,384,768]{2,1,0:T(8,128)(2,1)} %bitcast.65), dimensions={2,3,4} | broadcast | bytes 20054016 | tf_op jit(solution)/shard_map/stack | solution.py:65
  14.2 10.2 %all-to-all-start = ((bf16[16,1,2,384,768]{4,3,2,1,0:T(8,128)(2,1)}), bf16[16,1,2,384,768]{4,3,2,1,0:T(8,128)(2,1)}, u32[]{:S(2)}, u32[]{:S(2)}) async-start(bf16[16,1,2,384,768]{4,3,2,1,0:T(8,128)(2,1)} %stack.2), calls=%async_computation | async-start | bytes 37748736 | tf_op jit(solution)/shard_map/all_to_all | solution.py:65
  24.4 0.0 reduce-scatter.2.cloned.1.call-start
  24.4 430.7 %all-to-all-done = bf16[16,1,2,384,768]{4,3,2,1,0:T(8,128)(2,1)} async-done(((bf16[16,1,2,384,768]{4,3,2,1,0:T(8,128)(2,1)}), bf16[16,1,2,384,768]{4,3,2,1,0:T(8,128)(2,1)}, u32[]{:S(2)}, u32[]{:S(2)}) %all-to-all-start) | async-done | bytes 18874400 | tf_op jit(solution)/shard_map/all_to_all | solution.py:65
  455.1 9.8 %copy.75 = bf16[16,1,2,384,768]{4,3,0,2,1:T(8,128)(2,1)S(1)} copy(bf16[16,1,2,384,768]{4,3,2,1,0:T(8,128)(2,1)} %all-to-all-done) | data formatting | bytes 37748736 | tf_op jit(solution)/shard_map/all_to_all | solution.py:65
  464.9 0.0 copy-start.3
  464.9 0.0 copy-start.5
  464.9 6.6 %slice_bitcast_fusion = (bf16[6144,768]{1,0:T(8,128)(2,1)}, bf16[6144,768]{1,0:T(8,128)(2,1)}) fusion(bf16[1,2,6144,768]{3,2,1,0:T(8,128)(2,1)S(1)} %bitcast.55), kind=kLoop, calls=%fused_computation.24 | loop fusion | bytes 37748736 | tf_op jit(solution)/shard_map/squeeze | solution.py:68
  471.5 0.0 copy-done.3
  471.5 0.0 copy-done.5
  471.5 1.1 conditional.2
  471.5 0.1 broadcast.24.clone.1
  471.6 0.1 broadcast.24.clone
  471.7 0.9 broadcast.24
  472.6 0.3 copy.80
  472.9 0.3 copy.81
  473.1 1.3 collective-permute-start.1
  474.4 1.3 collective-permute-start
  475.7 42.7 %collective-permute-done.1 = bf16[512,768]{1,0:T(8,128)(2,1)S(1)} collective-permute-done((bf16[512,768]{1,0:T(8,128)(2,1)S(1)}, bf16[512,768]{1,0:T(8,128)(2,1)S(1)}, u32[]{:S(2)}, u32[]{:S(2)}) %collective-permute-start.1) | collective-permute-done | bytes 786464 | tf_op jit(solution)/shard_map/ppermute | solution.py:12
  518.5 16.9 %collective-permute-done = bf16[512,768]{1,0:T(8,128)(2,1)S(1)} collective-permute-done((bf16[512,768]{1,0:T(8,128)(2,1)S(1)}, bf16[512,768]{1,0:T(8,128)(2,1)S(1)}, u32[]{:S(2)}, u32[]{:S(2)}) %collective-permute-start) | collective-permute-done | bytes 786464 | tf_op jit(solution)/shard_map/ppermute | solution.py:12
  535.3 24.2 %conditional.3 = (bf16[512,6144]{1,0:T(8,128)(2,1)}) conditional(s32[]{:T(128)} %convert_element_type.36, (bf16[512,768]{1,0:T(8,128)(2,1)S(1)}, bf16[6144,768]{1,0:T(8,128)(2,1)}, bf16[512,768]{1,0:T(8,128)(2,1)S(1)}, bf16[6144,768]{1,0:T(8,128)(2,1)}) %tuple.21, (bf16[512,768]{0,1:T(8,128)(2,1)}, bf16[6144,768]{1,0:T(8,128)(2,1)}) %tuple.22), branch_computations={%region_5.6_spmd, %region_6.7_spmd} | conditional | flops 9669967872 | bytes 51904520 | solution.py:90
  535.3 11.6 %fusion.21 = f32[512,6144]{1,0:T(8,128)} fusion(bf16[512,768]{1,0:T(8,128)(2,1)S(1)} %get-tuple-element.38, bf16[6144,768]{1,0:T(8,128)(2,1)} %get-tuple-element.39), kind=kOutput, calls=%fused_computation.28 | convolution fusion | flops 4831838208 | bytes 22806528 | tf_op jit(solution)/shard_map/cond/branch_0_fun/dot_general | solution.py:57
  546.9 12.6 %convolution_add_fusion = bf16[512,6144]{1,0:T(8,128)(2,1)} fusion(f32[512,6144]{1,0:T(8,128)} %fusion.21, bf16[512,768]{1,0:T(8,128)(2,1)S(1)} %get-tuple-element.40, bf16[6144,768]{1,0:T(8,128)(2,1)} %get-tuple-element.41), kind=kOutput, calls=%fused_computation.23 | convolution fusion | flops 4838129664 | bytes 29097984 | tf_op jit(solution)/shard_map/cond/branch_0_fun/dot_general | solution.py:57
  559.5 0.0 reduce-scatter.2.cloned.1.call-update
  559.5 41.7 %reduce-scatter.2.cloned.1.call-done = bf16[512,768]{1,0:T(8,128)(2,1)} async-done(((bf16[512,6144]{1,0:T(8,128)(2,1)}), bf16[512,768]{1,0:T(8,128)(2,1)}) %reduce-scatter.2.cloned.1.call-update) | async-done | bytes 786448 | tf_op jit(solution)/shard_map/reduce_scatter | solution.py:95
Async XLA Ops:
  14.2 440.9 %all-to-all-start = ((bf16[16,1,2,384,768]{4,3,2,1,0:T(8,128)(2,1)}), bf16[16,1,2,384,768]{4,3,2,1,0:T(8,128)(2,1)}, u32[]{:S(2)}, u32[]{:S(2)}) async-start(bf16[16,1,2,384,768]{4,3,2,1,0:T(8,128)(2,1)} %stack.2), calls=%async_computation | async-start | bytes 37748736 | tf_op jit(solution)/shard_map/all_to_all | solution.py:65
  24.4 576.9 %reduce-scatter.2.cloned.1.call-start = ((), (), s32[]{:S(2)}) async-start(), calls=%async_computation.2 | async-start | bytes 7077888 | tf_op jit(solution)/shard_map/reduce_scatter | solution.py:95
  464.9 6.7 %copy-start.3 = (bf16[2,1,256,768]{3,2,1,0:T(8,128)(2,1)S(1)}, bf16[2,1,256,768]{3,2,1,0:T(8,128)(2,1)}, u32[]{:S(2)}) copy-start(bf16[2,1,256,768]{3,2,1,0:T(8,128)(2,1)} %param.13) | copy-start | bytes 2359300
  464.9 6.7 %copy-start.5 = (s32[2,1,256]{2,1,0:T(1,128)S(1)}, s32[2,1,256]{2,1,0:T(1,128)}, u32[]{:S(2)}) copy-start(s32[2,1,256]{2,1,0:T(1,128)} %param.14) | copy-start | bytes 6148
  473.1 45.3 %collective-permute-start.1 = (bf16[512,768]{1,0:T(8,128)(2,1)S(1)}, bf16[512,768]{1,0:T(8,128)(2,1)S(1)}, u32[]{:S(2)}, u32[]{:S(2)}) collective-permute-start(bf16[512,768]{1,0:T(8,128)(2,1)S(1)} %copy.81), channel_id=1, source_target_pairs={{128,0},{129,1},{130,2},{131,3},{132,4},{133,5},{134,6},{135,7},{1... | collective-permute-start | bytes 2359304 | tf_op jit(solution)/shard_map/ppermute | solution.py:12
  474.4 60.9 %collective-permute-start = (bf16[512,768]{1,0:T(8,128)(2,1)S(1)}, bf16[512,768]{1,0:T(8,128)(2,1)S(1)}, u32[]{:S(2)}, u32[]{:S(2)}) collective-permute-start(bf16[512,768]{1,0:T(8,128)(2,1)S(1)} %copy.80), channel_id=1, source_target_pairs={{128,0},{129,1},{130,2},{131,3},{132,4},{133,5},{134,6},{135,7},{1... | collective-permute-start | bytes 2359304 | tf_op jit(solution)/shard_map/ppermute | solution.py:12
Sparse Core Ops, SparseCore 0:
  559.6 41.5 reduce-scatter.1
